TPU v7x, 32 devices: a whole 2x2x4 slice. The times are simulated.
32 devices in a mesh: domain: 8 (over z, y), vec: 4 (over x, core).
Axes of the slice: x: 2, y: 2, z: 4, core: 2. Of those that a mesh axis runs over, the one named last changes fastest.
Arguments:
- vectors: float32 [4096, 512], P('domain', 'vec'), may hold values from -6 to 6
- hamiltonian: float32 [512, 128, 128], P('domain'), may hold values from -0.09375 to 0.09375
- tile_pairs: int32 [512, 2], P('domain'), may hold values from 0 to 31, as said below
- tile_counts: int32 [8], P('domain'), may hold values from 8 to 64, as said below
Outputs:
- filtered: float32 [4096, 512], P('domain', 'vec')
- gram: float32 [512, 512], P('vec')
Inputs may be any that keep to these rules, and one draw needn't show every extreme that they name: `tile_pairs`: slots k * 64 to (k + 1) * 64 - 1 have their row group r among groups k * 4 to (k + 1) * 4 - 1 and their column group c with r <= c <= min(k * 4 + 3 * 4 - 1, 31); pairs may repeat, and repeated blocks add. `tile_counts`: one domain index uses all 64 slots.
All inputs are finite; a program needn't handle non-finite values.
Results may differ from a plain program's by a relative error of at most 0.0003.
Values sent between devices are 32-bit elements; how exact they have to be, the bound alone decides.
A program may use at most 64 MiB of HBM per device.

v0:
```python
import jax
import jax.numpy as jnp
from jax import lax
from jax.sharding import PartitionSpec as P

TILE = 128
REACH = 2


center_shift = 1.0
half_width = 1.5


def from_behind(block, axis, distance):
    devices = range(lax.axis_size(axis))
    route = [(i - distance, i) for i in devices if i - distance in devices]
    return lax.ppermute(block, axis, route)


def local_products(own, window, tiles, row_loc, col_loc, count, groups):
    block_slots = 8
    width = own.shape[2]
    span = window.shape[0]
    n_blocks = (count + block_slots - 1) // block_slots

    def block_step(index, carry):
        rows_acc, back_acc = carry
        start = index * block_slots
        tile = lax.dynamic_slice_in_dim(tiles, start, block_slots, 0)
        rloc = lax.dynamic_slice_in_dim(row_loc, start, block_slots, 0)
        cloc = lax.dynamic_slice_in_dim(col_loc, start, block_slots, 0)
        used = (start + jnp.arange(block_slots, dtype=jnp.int32) < count).astype(jnp.float32)
        apart = (rloc != cloc).astype(jnp.float32)
        fwd = jnp.einsum("tij,tjc->tic", tile, window[cloc], precision=lax.Precision.HIGHEST)
        back = jnp.einsum("tji,tjc->tic", tile, own[rloc], precision=lax.Precision.HIGHEST)
        row_hot = (rloc[:, None] == jnp.arange(groups, dtype=jnp.int32)[None, :]).astype(
            jnp.float32
        ) * used[:, None]
        col_hot = (cloc[:, None] == jnp.arange(span, dtype=jnp.int32)[None, :]).astype(
            jnp.float32
        ) * (used * apart)[:, None]
        rows_acc = rows_acc + jnp.einsum(
            "tg,tic->gic", row_hot, fwd, precision=lax.Precision.HIGHEST
        )
        back_acc = back_acc + jnp.einsum(
            "tg,tic->gic", col_hot, back, precision=lax.Precision.HIGHEST
        )
        return (rows_acc, back_acc)

    start_rows = jnp.zeros((groups, TILE, width), jnp.float32)
    start_back = jnp.zeros((span, TILE, width), jnp.float32)
    return lax.fori_loop(0, n_blocks, block_step, (start_rows, start_back))


def apply_ham(block, tiles, row_loc, col_loc, count):
    groups = block.shape[0] // TILE
    width = block.shape[1]
    own = block.reshape(groups, TILE, width)
    pieces = [own]
    for step in range(1, REACH + 1):
        pieces.append(from_behind(own, "domain", -step))
    window = jnp.concatenate(pieces, 0)
    rows_acc, back_acc = local_products(own, window, tiles, row_loc, col_loc, count, groups)
    result = rows_acc + back_acc[:groups]
    for step in range(1, REACH + 1):
        result = result + from_behind(back_acc[step * groups : (step + 1) * groups], "domain", step)
    return result.reshape(groups * TILE, width)


def shards(vectors, hamiltonian, tile_pairs, tile_counts):
    groups = vectors.shape[0] // TILE
    base = lax.axis_index("domain") * groups
    count = tile_counts[0]
    diag = tile_pairs[:, 0] == tile_pairs[:, 1]
    tiles = jnp.where(
        diag[:, None, None], 0.5 * (hamiltonian + jnp.swapaxes(hamiltonian, 1, 2)), hamiltonian
    )
    row_loc = tile_pairs[:, 0] - base
    col_loc = tile_pairs[:, 1] - base
    second = (
        apply_ham(vectors, tiles, row_loc, col_loc, count) - center_shift * vectors
    ) / half_width
    third = (
        2.0
        * (apply_ham(second, tiles, row_loc, col_loc, count) - center_shift * second)
        / half_width
        - vectors
    )
    filtered = (
        2.0 * (apply_ham(third, tiles, row_loc, col_loc, count) - center_shift * third) / half_width
        - second
    )
    total_rows = vectors.shape[0] * lax.axis_size("domain")
    gathered = lax.all_gather(filtered, "vec", axis=1, tiled=True)
    partial_block = (
        jnp.dot(
            filtered.T,
            gathered,
            precision=lax.Precision.HIGHEST,
            preferred_element_type=jnp.float32,
        )
        / total_rows
    )
    gram = lax.psum(partial_block, "domain")
    return (filtered, gram)


def solution(mesh):
    in_specs = (P("domain", "vec"), P("domain", None, None), P("domain", None), P("domain"))
    out_specs = (P("domain", "vec"), P("vec", None))
    return jax.shard_map(shards, mesh=mesh, in_specs=in_specs, out_specs=out_specs, check_vma=False)
```

profile of v0, /device:TPU:0, one launch (start us, length us, event | category | flops | bytes accessed | tf_op | source)
XLA Modules:
  0.0 391.4 jit_solution(13187985193437510828)
XLA Ops:
  7.2 1.3 collective-permute-start.1
  8.5 1.3 collective-permute-start
  9.8 5.6 %copy.6 = f32[64,128,128]{1,2,0:T(8,128)} copy(f32[64,128,128]{2,1,0:T(8,128)} %param.11) | data formatting | bytes 8388608 | tf_op args[1]
  15.4 5.9 %fusion.61 = f32[64,128,128]{2,1,0:T(8,128)} fusion(f32[64,128,128]{2,1,0:T(8,128)} %param.11, f32[64,128,128]{1,2,0:T(8,128)} %copy.6, pred[64]{0:T(512)(128)(4,1)S(1)} %compare_bitcast_fusion), kind=kLoop, calls=%fused_computation.98 | loop fusion | flops 3145728 | bytes 12582976 | tf_op jit(solution)/shard_map/jit(_where)/select_n | solution.py:75
  22.3 24.5 %while.36 = (s32[]{:T(128)}, f32[4,128,128]{2,0,1:T(4,128)S(1)}, f32[12,128,128]{2,0,1:T(8,128)S(1)}, s32[]{:T(128)}, s32[64]{0:T(128)S(1)}, /*index=5*/s32[]{:T...) while((s32[]{:T(128)}, f32[4,128,128]{2,0,1:T(4,128)S(1)}, ...), condition=%wide.region_1.2_spmd, body=%wide.region_0.1_spmd.sunk | while | flops 428083552 | bytes 8397583 | solution.py:52
  22.3 0.7 compare_select_fusion.15
  23.6 1.7 fusion.116
  25.3 1.0 convolution_add_fusion.12
  26.9 2.1 fusion.117
  29.0 1.5 convolution_add_fusion.13
  31.8 1.7 fusion.116
  33.5 1.0 convolution_add_fusion.12
  35.1 2.1 fusion.117
  37.1 1.5 convolution_add_fusion.13
  40.0 1.7 fusion.116
  41.7 1.0 convolution_add_fusion.12
  43.2 2.1 fusion.117
  45.3 1.5 convolution_add_fusion.13
  46.9 1.3 collective-permute-start.3
  48.2 49.7 %collective-permute-start.2 = (f32[4,128,128]{2,0,1:T(4,128)S(1)}, f32[4,128,128]{2,0,1:T(4,128)S(1)}, u32[]{:S(2)}, u32[]{:S(2)}) collective-permute-start(f32[4,128,128]{2,0,1:T(4,128)S(1)} %get-tuple-element.252), channel_id=1, source_target_pairs={{0,4},{4,8},{8,12},{12,16},{16,20},{20,24},{24,28},{1,5},{5,9},{9,... | collective-permute-start | bytes 786440 | tf_op jit(solution)/shard_map/ppermute | solution.py:17
  98.0 5.0 %collective-permute-done.2 = f32[4,128,128]{2,0,1:T(4,128)S(1)} collective-permute-done((f32[4,128,128]{2,0,1:T(4,128)S(1)}, f32[4,128,128]{2,0,1:T(4,128)S(1)}, u32[]{:S(2)}, u32[]{:S(2)}) %collective-permute-start.2) | collective-permute-done | bytes 262176 | tf_op jit(solution)/shard_map/ppermute | solution.py:17
  103.1 1.3 collective-permute-start.5
  104.4 1.3 collective-permute-start.4
  105.7 12.3 %collective-permute-done.5 = f32[4,128,128]{2,1,0:T(8,128)S(1)} collective-permute-done((f32[4,128,128]{2,1,0:T(8,128)S(1)}, f32[4,128,128]{2,1,0:T(8,128)S(1)}, u32[]{:S(2)}, u32[]{:S(2)}) %collective-permute-start.5) | collective-permute-done | bytes 262176 | tf_op jit(solution)/shard_map/ppermute | solution.py:17
  118.3 24.5 %while.37 = (s32[]{:T(128)}, f32[4,128,128]{2,0,1:T(4,128)S(1)}, f32[12,128,128]{2,0,1:T(8,128)S(1)}, s32[]{:T(128)}, s32[64]{0:T(128)S(1)}, /*index=5*/s32[]{:T...) while((s32[]{:T(128)}, f32[4,128,128]{2,0,1:T(4,128)S(1)}, ...), condition=%wide.region_3.4_spmd, body=%wide.region_2.3_spmd.sunk | while | flops 428083552 | bytes 8397583 | solution.py:52
  119.6 1.7 fusion.126
  121.3 1.0 convolution_add_fusion.14
  122.9 2.1 fusion.127
  124.9 1.5 convolution_add_fusion.15
  127.8 1.7 fusion.126
  129.5 1.0 convolution_add_fusion.14
  131.0 2.1 fusion.127
  133.1 1.5 convolution_add_fusion.15
  136.0 1.7 fusion.126
  137.7 1.0 convolution_add_fusion.14
  139.2 2.1 fusion.127
  141.3 1.5 convolution_add_fusion.15
  142.9 1.3 collective-permute-start.7
  144.2 50.2 %collective-permute-start.6 = (f32[4,128,128]{2,0,1:T(4,128)S(1)}, f32[4,128,128]{2,0,1:T(4,128)S(1)}, u32[]{:S(2)}, u32[]{:S(2)}) collective-permute-start(f32[4,128,128]{2,0,1:T(4,128)S(1)} %get-tuple-element.250), channel_id=1, source_target_pairs={{0,4},{4,8},{8,12},{12,16},{16,20},{20,24},{24,28},{1,5},{5,9},{9,... | collective-permute-start | bytes 786440 | tf_op jit(solution)/shard_map/ppermute | solution.py:17
  194.4 3.8 collective-permute-done.6
  198.5 1.3 collective-permute-start.9
  199.8 1.3 collective-permute-start.8
  201.1 10.5 %collective-permute-done.9 = f32[4,128,128]{2,1,0:T(8,128)S(1)} collective-permute-done((f32[4,128,128]{2,1,0:T(8,128)S(1)}, f32[4,128,128]{2,1,0:T(8,128)S(1)}, u32[]{:S(2)}, u32[]{:S(2)}) %collective-permute-start.9) | collective-permute-done | bytes 262176 | tf_op jit(solution)/shard_map/ppermute | solution.py:17
  211.8 24.7 %while.38 = (s32[]{:T(128)}, f32[4,128,128]{2,0,1:T(4,128)S(1)}, f32[12,128,128]{2,0,1:T(8,128)S(1)}, s32[]{:T(128)}, s32[64]{0:T(128)S(1)}, /*index=5*/s32[]{:T...) while((s32[]{:T(128)}, f32[4,128,128]{2,0,1:T(4,128)S(1)}, ...), condition=%wide.region_5.6_spmd, body=%wide.region_4.5_spmd.sunk | while | flops 428083552 | bytes 8397583 | solution.py:52
  213.3 1.7 fusion.136
  215.0 1.0 convolution_add_fusion.16
  216.6 2.1 fusion.137
  218.7 1.5 convolution_add_fusion.17
  221.5 1.7 fusion.136
  223.2 1.0 convolution_add_fusion.16
  224.8 2.1 fusion.137
  226.8 1.5 convolution_add_fusion.17
  229.7 1.7 fusion.136
  231.4 1.0 convolution_add_fusion.16
  232.9 2.1 fusion.137
  235.0 1.5 convolution_add_fusion.17
  236.6 1.3 collective-permute-start.11
  237.9 49.4 %collective-permute-start.10 = (f32[4,128,128]{2,0,1:T(4,128)S(1)}, f32[4,128,128]{2,0,1:T(4,128)S(1)}, u32[]{:S(2)}, u32[]{:S(2)}) collective-permute-start(f32[4,128,128]{2,0,1:T(4,128)S(1)} %get-tuple-element.248), channel_id=1, source_target_pairs={{0,4},{4,8},{8,12},{12,16},{16,20},{20,24},{24,28},{1,5},{5,9},{9,... | collective-permute-start | bytes 786440 | tf_op jit(solution)/shard_map/ppermute | solution.py:17
  287.4 3.8 collective-permute-done.10
  291.3 0.7 fusion.63
  292.2 15.7 %all-gather.2.cloned.1.call-done = f32[512,512]{1,0:T(8,128)} async-done(((f32[512,128]{1,0:T(8,128)}), f32[512,512]{1,0:T(8,128)}) %all-gather.2.cloned.1.call-update) | async-done | bytes 1048592 | tf_op jit(solution)/shard_map/all_gather | solution.py:94
  307.9 2.8 convolution_multiply_fusion
  310.7 72.2 %all-reduce.2.cloned.1.call-done = f32[128,512]{1,0:T(8,128)} async-done(((f32[128,512]{1,0:T(8,128)}), f32[128,512]{1,0:T(8,128)}) %all-reduce.2.cloned.1.call-update) | async-done | bytes 262160 | tf_op jit(solution)/shard_map/psum | solution.py:104
  382.9 1.7 copy.69
  (90 shorter events, 17.8 us)
Async XLA Ops:
  7.2 300.7 %all-gather.2.cloned.1.call-start = ((), (), s32[]{:S(2)}) async-start(), calls=%async_computation | async-start | bytes 1310720 | tf_op jit(solution)/shard_map/all_gather | solution.py:94
  7.2 8.2 %copy-start.1 = (s32[64,2]{0,1:T(2,128)S(1)}, s32[64,2]{0,1:T(2,128)}, u32[]{:S(2)}) copy-start(s32[64,2]{0,1:T(2,128)} %param.12) | copy-start | bytes 1540
  7.2 14.9 %collective-permute-start.1 = (f32[4,128,128]{2,1,0:T(8,128)}, f32[4,128,128]{2,1,0:T(8,128)S(1)}, u32[]{:S(2)}, u32[]{:S(2)}) collective-permute-start(f32[4,128,128]{2,1,0:T(8,128)} %bitcast.89), channel_id=1, source_target_pairs={{8,0},{12,4},{16,8},{20,12},{24,16},{28,20},{9,1},{13,5},{17,9},{2... | collective-permute-start | bytes 786440 | tf_op jit(solution)/shard_map/ppermute | solution.py:17
  8.5 13.6 %collective-permute-start = (f32[4,128,128]{2,1,0:T(8,128)}, f32[4,128,128]{2,1,0:T(8,128)S(1)}, u32[]{:S(2)}, u32[]{:S(2)}) collective-permute-start(f32[4,128,128]{2,1,0:T(8,128)} %bitcast.90), channel_id=1, source_target_pairs={{4,0},{8,4},{12,8},{16,12},{20,16},{24,20},{28,24},{5,1},{9,5},{13... | collective-permute-start | bytes 786440 | tf_op jit(solution)/shard_map/ppermute | solution.py:17
  15.4 6.7 %copy-start = (f32[512,128]{1,0:T(8,128)S(1)}, f32[512,128]{1,0:T(8,128)}, u32[]{:S(2)}) copy-start(f32[512,128]{1,0:T(8,128)} %param.10) | copy-start | bytes 786436
  46.9 51.1 %collective-permute-start.3 = (f32[4,128,128]{2,0,1:T(4,128)S(1)}, f32[4,128,128]{2,0,1:T(4,128)S(1)}, u32[]{:S(2)}, u32[]{:S(2)}) collective-permute-start(f32[4,128,128]{2,0,1:T(4,128)S(1)} %get-tuple-element.253), channel_id=1, source_target_pairs={{0,8},{4,12},{8,16},{12,20},{16,24},{20,28},{1,9},{5,13},{9,17},{1... | collective-permute-start | bytes 786440 | tf_op jit(solution)/shard_map/ppermute | solution.py:17
  48.2 54.7 %collective-permute-start.2 = (f32[4,128,128]{2,0,1:T(4,128)S(1)}, f32[4,128,128]{2,0,1:T(4,128)S(1)}, u32[]{:S(2)}, u32[]{:S(2)}) collective-permute-start(f32[4,128,128]{2,0,1:T(4,128)S(1)} %get-tuple-element.252), channel_id=1, source_target_pairs={{0,4},{4,8},{8,12},{12,16},{16,20},{20,24},{24,28},{1,5},{5,9},{9,... | collective-permute-start | bytes 786440 | tf_op jit(solution)/shard_map/ppermute | solution.py:17
  103.1 14.9 %collective-permute-start.5 = (f32[4,128,128]{2,1,0:T(8,128)S(1)}, f32[4,128,128]{2,1,0:T(8,128)S(1)}, u32[]{:S(2)}, u32[]{:S(2)}) collective-permute-start(f32[4,128,128]{2,1,0:T(8,128)S(1)} %bitcast.83), channel_id=1, source_target_pairs={{8,0},{12,4},{16,8},{20,12},{24,16},{28,20},{9,1},{13,5},{17,9},{2... | collective-permute-start | bytes 786440 | tf_op jit(solution)/shard_map/ppermute | solution.py:17
  104.4 13.6 %collective-permute-start.4 = (f32[4,128,128]{2,1,0:T(8,128)S(1)}, f32[4,128,128]{2,1,0:T(8,128)S(1)}, u32[]{:S(2)}, u32[]{:S(2)}) collective-permute-start(f32[4,128,128]{2,1,0:T(8,128)S(1)} %bitcast.84), channel_id=1, source_target_pairs={{4,0},{8,4},{12,8},{16,12},{20,16},{24,20},{28,24},{5,1},{9,5},{13... | collective-permute-start | bytes 786440 | tf_op jit(solution)/shard_map/ppermute | solution.py:17
  142.9 51.5 %collective-permute-start.7 = (f32[4,128,128]{2,0,1:T(4,128)S(1)}, f32[4,128,128]{2,0,1:T(4,128)S(1)}, u32[]{:S(2)}, u32[]{:S(2)}) collective-permute-start(f32[4,128,128]{2,0,1:T(4,128)S(1)} %get-tuple-element.251), channel_id=1, source_target_pairs={{0,8},{4,12},{8,16},{12,20},{16,24},{20,28},{1,9},{5,13},{9,17},{1... | collective-permute-start | bytes 786440 | tf_op jit(solution)/shard_map/ppermute | solution.py:17
  144.2 54.1 %collective-permute-start.6 = (f32[4,128,128]{2,0,1:T(4,128)S(1)}, f32[4,128,128]{2,0,1:T(4,128)S(1)}, u32[]{:S(2)}, u32[]{:S(2)}) collective-permute-start(f32[4,128,128]{2,0,1:T(4,128)S(1)} %get-tuple-element.250), channel_id=1, source_target_pairs={{0,4},{4,8},{8,12},{12,16},{16,20},{20,24},{24,28},{1,5},{5,9},{9,... | collective-permute-start | bytes 786440 | tf_op jit(solution)/shard_map/ppermute | solution.py:17
  198.5 13.1 %collective-permute-start.9 = (f32[4,128,128]{2,1,0:T(8,128)S(1)}, f32[4,128,128]{2,1,0:T(8,128)S(1)}, u32[]{:S(2)}, u32[]{:S(2)}) collective-permute-start(f32[4,128,128]{2,1,0:T(8,128)S(1)} %bitcast.95), channel_id=1, source_target_pairs={{8,0},{12,4},{16,8},{20,12},{24,16},{28,20},{9,1},{13,5},{17,9},{2... | collective-permute-start | bytes 786440 | tf_op jit(solution)/shard_map/ppermute | solution.py:17
  199.8 11.8 %collective-permute-start.8 = (f32[4,128,128]{2,1,0:T(8,128)S(1)}, f32[4,128,128]{2,1,0:T(8,128)S(1)}, u32[]{:S(2)}, u32[]{:S(2)}) collective-permute-start(f32[4,128,128]{2,1,0:T(8,128)S(1)} %bitcast.96), channel_id=1, source_target_pairs={{4,0},{8,4},{12,8},{16,12},{20,16},{24,20},{28,24},{5,1},{9,5},{13... | collective-permute-start | bytes 786440 | tf_op jit(solution)/shard_map/ppermute | solution.py:17
  236.6 50.7 %collective-permute-start.11 = (f32[4,128,128]{2,0,1:T(4,128)S(1)}, f32[4,128,128]{2,0,1:T(4,128)S(1)}, u32[]{:S(2)}, u32[]{:S(2)}) collective-permute-start(f32[4,128,128]{2,0,1:T(4,128)S(1)} %get-tuple-element.249), channel_id=1, source_target_pairs={{0,8},{4,12},{8,16},{12,20},{16,24},{20,28},{1,9},{5,13},{9,17},{1... | collective-permute-start | bytes 786440 | tf_op jit(solution)/shard_map/ppermute | solution.py:17
  237.9 53.3 %collective-permute-start.10 = (f32[4,128,128]{2,0,1:T(4,128)S(1)}, f32[4,128,128]{2,0,1:T(4,128)S(1)}, u32[]{:S(2)}, u32[]{:S(2)}) collective-permute-start(f32[4,128,128]{2,0,1:T(4,128)S(1)} %get-tuple-element.248), channel_id=1, source_target_pairs={{0,4},{4,8},{8,12},{12,16},{16,20},{20,24},{24,28},{1,5},{5,9},{9,... | collective-permute-start | bytes 786440 | tf_op jit(solution)/shard_map/ppermute | solution.py:17
  292.1 90.8 %all-reduce.2.cloned.1.call-start = ((), (), s32[]{:S(2)}) async-start(), calls=%async_computation.1 | async-start | bytes 524288 | tf_op jit(solution)/shard_map/psum | solution.py:104
Sparse Core Ops, SparseCore 0:
  292.2 15.6 all-gather.1
  311.8 71.0 all-reduce.1
where the time goes:
time: 394 us; the launch traced here: 391 us
  starting transfers between devices  161 us (41%)
  waiting for transfers between devices  124 us (31%)
  matrix products  58.6 us (15%)
  local copies, waits for them, and re-layouts  18.4 us (5%)
  between operations  15 us (4%)
  other arithmetic  14 us (4%)
    ppermute x12, starting transfers between devices, from_behind(): return lax.ppermute(block, axis, route)  161 us
    psum x1, waiting for transfers between devices, shards(): gram = lax.psum(partial_block, 'domain')  72.2 us
    ppermute x12, waiting for transfers between devices, from_behind(): return lax.ppermute(block, axis, route)  35.6 us
    dot_general x9, matrix products, block_step(): jnp.einsum('tji,tjc->tic', tile, own[rloc], precision=lax.Precision.HIGHEST)  18.5 us
    all_gather x1, waiting for transfers between devices, shards(): gathered = lax.all_gather(filtered, 'vec', axis=1, tiled=True)  15.7 us
    dot_general x9, matrix products, block_step(): jnp.einsum('tij,tjc->tic', tile, window[cloc], precision=lax.Precision.HI...  15.2 us
    dot_general x9, matrix products, block_step(): jnp.einsum('tg,tic->gic', col_hot, back, precision=lax.Precision.HIGHEST)  13.5 us
    dot_general x9, matrix products, block_step(): jnp.einsum('tg,tic->gic', row_hot, fwd, precision=lax.Precision.HIGHEST)  8.57 us
  transfers between devices with their start and end apart: 14, of which 7 were waited for; matrix products, arithmetic and copies ran while one was open for 3% of the time, Pallas kernels for 0%

commit v1 on v0

v1 whole, which is shorter than its diff:
```python
import functools

import jax
import jax.numpy as jnp
from jax import lax
from jax.experimental import pallas as pl
from jax.experimental.pallas import tpu as pltpu
from jax.sharding import PartitionSpec as P

TILE = 128
REACH = 2
CHUNK = 8

center_shift = 1.0
half_width = 1.5

F32 = jnp.float32
BF16 = jnp.bfloat16


def densify_kernel(groups, pairs_ref, count_ref, ham_ref, dense_ref, tiles, sems):
    slots = ham_ref.shape[0]
    chunk = CHUNK if slots % CHUNK == 0 else slots
    count = count_ref[0]
    base = lax.axis_index("domain") * groups

    def copy(index):
        part = pl.ds(index * chunk, chunk)
        return pltpu.make_async_copy(ham_ref.at[part], tiles.at[part], sems.at[index])

    for index in range(slots // chunk):

        @pl.when(count > index * chunk)
        def _():
            copy(index).start()

    dense_ref[...] = jnp.zeros_like(dense_ref)

    def add(slot, carry):
        row = pairs_ref[slot, 0]
        col = pairs_ref[slot, 1]
        scale = jnp.where(row == col, 0.5, 1.0).astype(F32)
        rows = pl.ds(pl.multiple_of((row - base) * TILE, TILE), TILE)
        cols = pl.ds(pl.multiple_of((col - base) * TILE, TILE), TILE)
        dense_ref[rows, cols] += tiles[slot] * scale
        return carry

    for index in range(slots // chunk):

        @pl.when(count > index * chunk)
        def _():
            copy(index).wait()
            lax.fori_loop(index * chunk, jnp.minimum(count, (index + 1) * chunk), add, 0)


def densify(hamiltonian, tile_pairs, tile_counts, groups):
    slots = hamiltonian.shape[0]
    return pl.pallas_call(
        functools.partial(densify_kernel, groups),
        out_shape=jax.ShapeDtypeStruct((groups * TILE, (REACH + 1) * groups * TILE), F32),
        in_specs=[
            pl.BlockSpec(memory_space=pltpu.SMEM),
            pl.BlockSpec(memory_space=pltpu.SMEM),
            pl.BlockSpec(memory_space=pl.ANY),
        ],
        out_specs=pl.BlockSpec(memory_space=pltpu.VMEM),
        scratch_shapes=[
            pltpu.VMEM(hamiltonian.shape, F32),
            pltpu.SemaphoreType.DMA((slots // CHUNK + 1,)),
        ],
        name="densify",
    )(tile_pairs, tile_counts, hamiltonian)


def halves(value):
    high = value.astype(BF16)
    low = (value - high.astype(F32)).astype(BF16)
    return high, low


def stacked(value):
    return jnp.concatenate(halves(value), 1)


def product(high, low, both):
    wide = jnp.dot(high, both, preferred_element_type=F32)
    wide = wide + jnp.dot(low, both, preferred_element_type=F32)
    width = both.shape[1] // 2
    return wide[:, :width] + wide[:, width:]


def filter_kernel(n, m, with_gram, x_ref, dense_hbm, *refs):
    if with_gram:
        f_ref, g_ref, *refs = refs
    else:
        f_ref, *refs = refs
    (dense, fwd_h, fwd_l, back_h, back_l, both, acc, x1_ref, x2_ref, in_x, in_b, out_b) = refs[:12]
    (load_sem, xs_sem, xr_sem, bs_sem, br_sem) = refs[12:17]
    me = lax.axis_index("domain")
    mine = lax.axis_index("vec")
    rows, width = x_ref.shape

    load = pltpu.make_async_copy(dense_hbm, dense, load_sem)
    load.start()

    barrier = pltpu.get_barrier_semaphore()
    if with_gram:
        for d in range(1, n):
            pl.semaphore_signal(barrier, inc=1, device_id={"domain": (me + d) % n})
        for d in range(1, m):
            pl.semaphore_signal(barrier, inc=1, device_id={"vec": (mine + d) % m})
        pl.semaphore_wait(barrier, n - 1 + m - 1)
    else:
        for d in range(1, REACH + 1):

            @pl.when(me >= d)
            def _():
                pl.semaphore_signal(barrier, inc=1, device_id={"domain": me - d})

            @pl.when(me + d < n)
            def _():
                pl.semaphore_signal(barrier, inc=1, device_id={"domain": me + d})

        for d in range(1, REACH + 1):

            @pl.when(me >= d)
            def _():
                pl.semaphore_wait(barrier, 1)

            @pl.when(me + d < n)
            def _():
                pl.semaphore_wait(barrier, 1)

    def x_copy(step, d, source):
        return pltpu.make_async_remote_copy(
            src_ref=source,
            dst_ref=in_x.at[step, d - 1],
            send_sem=xs_sem.at[step, d - 1],
            recv_sem=xr_sem.at[step, d - 1],
            device_id={"domain": me - d},
        )

    def b_copy(step, d):
        return pltpu.make_async_remote_copy(
            src_ref=out_b.at[step, d - 1],
            dst_ref=in_b.at[step, d - 1],
            send_sem=bs_sem.at[step, d - 1],
            recv_sem=br_sem.at[step, d - 1],
            device_id={"domain": me + d},
        )

    sources = (x_ref, x1_ref, x2_ref)
    for step in range(3):
        source = sources[step]
        for d in range(1, REACH + 1):

            @pl.when(me >= d)
            def _():
                x_copy(step, d, source).start()

        both[...] = stacked(source[...])
        if step == 0:
            load.wait()
        for d in range(1, REACH + 1):

            @pl.when(me + d < n)
            def _():
                if step == 0:
                    block = dense[:, d * rows : (d + 1) * rows]
                    back_h[d - 1], back_l[d - 1] = halves(block.T)
                out_b[step, d - 1] = product(back_h[d - 1], back_l[d - 1], both[...])
                b_copy(step, d).start()

        if step == 0:
            block = dense[:, :rows]
            fwd_h[0], fwd_l[0] = halves(block + block.T)
            for d in range(1, REACH + 1):
                fwd_h[d], fwd_l[d] = halves(dense[:, d * rows : (d + 1) * rows])
        acc[...] = product(fwd_h[0], fwd_l[0], both[...])
        for d in range(1, REACH + 1):

            @pl.when(me + d < n)
            def _():
                x_copy(step, d, source).wait_recv()
                acc[...] += product(fwd_h[d], fwd_l[d], stacked(in_x[step, d - 1]))

        for d in range(1, REACH + 1):

            @pl.when(me >= d)
            def _():
                b_copy(step, d).wait_recv()
                acc[...] += in_b[step, d - 1]

        if step == 0:
            x1_ref[...] = (acc[...] - center_shift * x_ref[...]) / half_width
        elif step == 1:
            x2_ref[...] = 2.0 * (acc[...] - center_shift * x1_ref[...]) / half_width - x_ref[...]
        else:
            f_ref[...] = 2.0 * (acc[...] - center_shift * x2_ref[...]) / half_width - x1_ref[...]

    if with_gram:
        (in_f, part, in_g, g_mine) = refs[17:21]
        (fs_sem, fr_sem, gs_sem, gr_sem, hs_sem, hr_sem) = refs[21:]
        far = (mine + 2) % 4
        near = mine + 1 - 2 * (mine % 2)
        cross = (near + 2) % 4

        def f_copy(index, source, target):
            return pltpu.make_async_remote_copy(
                src_ref=source,
                dst_ref=in_f.at[index],
                send_sem=fs_sem.at[index],
                recv_sem=fr_sem.at[index],
                device_id={"vec": target},
            )

        to_far = f_copy(0, f_ref, far)
        to_near = f_copy(1, f_ref, near)
        relay = f_copy(2, in_f.at[0], near)
        to_far.start()
        to_near.start()
        left_h, left_l = halves(f_ref[...].T)
        back_h[0, :width], back_l[0, :width] = left_h, left_l
        total = rows * n

        def gram_block(value, owner):
            block = product(back_h[0, :width], back_l[0, :width], stacked(value)) / total
            part[:, pl.ds(pl.multiple_of(owner * width, width), width)] = block

        gram_block(f_ref[...], mine)
        to_near.wait_recv()
        gram_block(in_f[1], near)
        to_far.wait_recv()
        relay.start()
        gram_block(in_f[0], far)
        relay.wait_recv()
        gram_block(in_f[2], cross)

        piece = width // n

        def rows_of(owner):
            return pl.ds(pl.multiple_of(owner * piece, piece), piece)

        def g_copy(d):
            peer = (me + d) % n
            return pltpu.make_async_remote_copy(
                src_ref=part.at[rows_of(peer)],
                dst_ref=in_g.at[d],
                send_sem=gs_sem.at[d],
                recv_sem=gr_sem.at[d],
                device_id={"domain": peer},
            )

        def h_copy(d, owner):
            return pltpu.make_async_remote_copy(
                src_ref=g_mine,
                dst_ref=g_ref.at[rows_of(owner)],
                send_sem=hs_sem.at[d],
                recv_sem=hr_sem.at[d],
                device_id={"domain": (me + d) % n},
            )

        for d in range(1, n):
            g_copy(d).start()
        block = part[rows_of(me)]
        for d in range(1, n):
            g_copy(d).wait_recv()
            block = block + in_g[d]
        g_mine[...] = block
        for d in range(1, n):
            h_copy(d, me).start()
        g_ref[rows_of(me)] = block
        for d in range(1, n):
            h_copy(d, (me + n - d) % n).wait_recv()
        to_far.wait_send()
        to_near.wait_send()
        relay.wait_send()
        for d in range(1, n):
            g_copy(d).wait_send()
            h_copy(d, me).wait_send()

    for step in range(3):
        for d in range(1, REACH + 1):

            @pl.when(me >= d)
            def _():
                x_copy(step, d, sources[step]).wait_send()

            @pl.when(me + d < n)
            def _():
                b_copy(step, d).wait_send()


def shards(vectors, hamiltonian, tile_pairs, tile_counts):
    n = lax.axis_size("domain")
    m = lax.axis_size("vec")
    rows, width = vectors.shape
    groups = rows // TILE
    dense = densify(hamiltonian, tile_pairs, tile_counts, groups)
    with_gram = m == 4 and width % (8 * n) == 0
    dma = pltpu.SemaphoreType.DMA
    out_shape = [jax.ShapeDtypeStruct((rows, width), F32)]
    scratch = [
        pltpu.VMEM(dense.shape, F32),
        pltpu.VMEM((REACH + 1, rows, rows), BF16),
        pltpu.VMEM((REACH + 1, rows, rows), BF16),
        pltpu.VMEM((REACH, rows, rows), BF16),
        pltpu.VMEM((REACH, rows, rows), BF16),
        pltpu.VMEM((rows, 2 * width), BF16),
        pltpu.VMEM((rows, width), F32),
        pltpu.VMEM((rows, width), F32),
        pltpu.VMEM((rows, width), F32),
        pltpu.VMEM((3, REACH, rows, width), F32),
        pltpu.VMEM((3, REACH, rows, width), F32),
        pltpu.VMEM((3, REACH, rows, width), F32),
        dma,
        dma((3, REACH)),
        dma((3, REACH)),
        dma((3, REACH)),
        dma((3, REACH)),
    ]
    if with_gram:
        out_shape.append(jax.ShapeDtypeStruct((width, m * width), F32))
        scratch += [
            pltpu.VMEM((3, rows, width), F32),
            pltpu.VMEM((width, m * width), F32),
            pltpu.VMEM((n, width // n, m * width), F32),
            pltpu.VMEM((width // n, m * width), F32),
            dma((3,)),
            dma((3,)),
            dma((n,)),
            dma((n,)),
            dma((n,)),
            dma((n,)),
        ]
    outs = pl.pallas_call(
        functools.partial(filter_kernel, n, m, with_gram),
        out_shape=out_shape,
        in_specs=[pl.BlockSpec(memory_space=pltpu.VMEM), pl.BlockSpec(memory_space=pl.ANY)],
        out_specs=[pl.BlockSpec(memory_space=pltpu.VMEM)] * len(out_shape),
        scratch_shapes=scratch,
        compiler_params=pltpu.CompilerParams(
            collective_id=0, has_side_effects=True, vmem_limit_bytes=50 * 2**20
        ),
        name="chebyshev",
    )(vectors, dense)
    if with_gram:
        return tuple(outs)
    (filtered,) = outs
    gathered = lax.all_gather(filtered, "vec", axis=1, tiled=True)
    partial_block = jnp.dot(
        filtered.T, gathered, precision=lax.Precision.HIGHEST, preferred_element_type=F32
    ) / (rows * n)
    return (filtered, lax.psum(partial_block, "domain"))


def solution(mesh):
    in_specs = (P("domain", "vec"), P("domain", None, None), P("domain", None), P("domain"))
    out_specs = (P("domain", "vec"), P("vec", None))
    return jax.shard_map(shards, mesh=mesh, in_specs=in_specs, out_specs=out_specs, check_vma=False)
```

time: 394 us -> 79.6 us (0.20)
  starting transfers between devices: 161 us -> 0 us
  waiting for transfers between devices: 124 us -> 0 us
  Pallas kernels: 0 us -> 72.2 us
  matrix products: 58.6 us -> 0 us
  other arithmetic: 14 us -> 0 us
  local copies, waits for them, and re-layouts: 18.4 us -> 4.68 us
  between operations: 15 us -> 1.36 us
    ppermute x12 -> x0, starting transfers between devices: 161 us -> none  [from_behind(): return lax.ppermute(block, axis, route)]
    pallas_call x0 -> x2, Pallas kernels: none -> 72.2 us  [the longest x1 67.6 us: shards(): pl.pallas_call(functools.partial(filter_kernel, n, m, with_gram), out_sha...]
    psum x1 -> x0, waiting for transfers between devices: 72.2 us -> none  [shards(): gram = lax.psum(partial_block, 'domain')]
    dot_general x37 -> x0, matrix products: 58.6 us -> none  [the longest x9 18.5 us: block_step(): jnp.einsum('tji,tjc->tic', tile, own[rloc], precision=lax.Precision.HIGHEST)]
    ppermute x12 -> x0, waiting for transfers between devices: 35.6 us -> none  [from_behind(): return lax.ppermute(block, axis, route)]
    all_gather x1 -> x0, waiting for transfers between devices: 15.7 us -> none  [shards(): gathered = lax.all_gather(filtered, 'vec', axis=1, tiled=True)]
    gather x18 -> x0, local copies, waits for them, and re-layouts: 10.5 us -> none  [the longest x9 5.24 us: block_step(): own[rloc]]
    mul x9 -> x0, other arithmetic: 6.52 us -> none  [block_step(): used * apart]
  transfers between devices with their start and end apart: 14 -> 0, of which waited for: 7 -> 0; matrix products, arithmetic and copies ran while one was open for 3% -> 0% of each run, Pallas kernels for 0% -> 0%
where the time goes in v1:
time: 79.6 us; the launch traced here: 78.3 us
  Pallas kernels  72.2 us (91%)
  local copies, waits for them, and re-layouts  4.68 us (6%)
  between operations  1.36 us (2%)
    pallas_call x1, Pallas kernels, shards(): pl.pallas_call(functools.partial(filter_kernel, n, m, with_gram), out_sha...  67.6 us
    unnamed x7, local copies, waits for them, and re-layouts  4.68 us
    pallas_call x1, Pallas kernels, densify(): pl.pallas_call(functools.partial(densify_kernel, groups), out_shape=jax.S...  4.58 us

profile of v1, /device:TPU:0, one launch (start us, length us, event | category | flops | bytes accessed | tf_op | source)
XLA Modules:
  0.0 78.3 jit_solution(5084209263753249682)
XLA Ops:
  0.6 0.0 copy-start.1
  1.3 1.4 %copy.6.pairs_ref = s32[64,2]{1,0:T(8,128)} copy(s32[64,2]{0,1:T(2,128)} %param.6) | data formatting | bytes 1024 | tf_op args[2]
  2.7 4.6 %densify.1.dense_hbm = f32[512,1536]{1,0:T(8,128)} custom-call(s32[64,2]{1,0:T(8,128)} %copy.6.pairs_ref, s32[1]{0:T(128)S(6)} %copy.9.count_ref, f32[64,128,128]{2,1,0:T(8,128)} %ham_ref.1), custom_call_target="tpu_custom_call" | custom-call | tf_op jit(solution)/shard_map/densify/pallas_call | solution.py:58
  7.3 0.0 copy-done.1
  7.3 0.0 copy-start
  7.3 1.9 %copy-done = f32[512,1536]{1,0:T(8,128)S(1)} copy-done((f32[512,1536]{1,0:T(8,128)S(1)}, f32[512,1536]{1,0:T(8,128)}, u32[]{:S(2)}) %copy-start) | copy-done | bytes 3145752
  9.2 67.6 %chebyshev.1 = (f32[512,128]{1,0:T(8,128)S(1)}, f32[128,512]{1,0:T(8,128)S(1)}) custom-call(f32[512,128]{1,0:T(8,128)S(1)} %copy-done.1, f32[512,1536]{1,0:T(8,128)S(1)} %copy-done), custom_call_target="tpu_custom_call" | custom-call | tf_op jit(solution)/shard_map/chebyshev/pallas_call | solution.py:336
  76.9 0.7 copy.10
  77.6 0.7 copy.11
Async XLA Ops:
  0.6 6.7 %copy-start.1 = (f32[512,128]{1,0:T(8,128)S(1)}, f32[512,128]{1,0:T(8,128)}, u32[]{:S(2)}) copy-start(f32[512,128]{1,0:T(8,128)} %x_ref.1) | copy-start | bytes 786436
  7.3 1.9 %copy-start = (f32[512,1536]{1,0:T(8,128)S(1)}, f32[512,1536]{1,0:T(8,128)}, u32[]{:S(2)}) copy-start(f32[512,1536]{1,0:T(8,128)} %densify.1.dense_hbm) | copy-start | bytes 9437188

commit v2 on v1

v2 whole, which is shorter than its diff:
```python
import functools

import jax
import jax.numpy as jnp
from jax import lax
from jax.experimental import pallas as pl
from jax.experimental.pallas import tpu as pltpu
from jax.sharding import PartitionSpec as P

TILE = 128
REACH = 2

center_shift = 1.0
half_width = 1.5

F32 = jnp.float32
BF16 = jnp.bfloat16


def index_kernel(groups, span, pairs_ref, count_ref, before_ref, last_ref):
    slots = pairs_ref.shape[1]
    count = count_ref[0]
    base = lax.axis_index("domain") * groups

    def clear(block, carry):
        last_ref[block] = -1
        return carry

    def chain(slot, carry):
        block = (pairs_ref[0, slot] - base) * span + pairs_ref[1, slot] - base
        before_ref[slot] = last_ref[block]
        last_ref[block] = slot
        return carry

    def skip(slot, carry):
        before_ref[slot] = -1
        return carry

    lax.fori_loop(0, groups * span, clear, 0)
    lax.fori_loop(0, count, chain, 0)
    lax.fori_loop(count, slots, skip, 0)


def index_slots(tile_pairs, tile_counts, groups):
    span = (REACH + 1) * groups
    smem = pl.BlockSpec(memory_space=pltpu.SMEM)
    return pl.pallas_call(
        functools.partial(index_kernel, groups, span),
        out_shape=[
            jax.ShapeDtypeStruct((tile_pairs.shape[0],), jnp.int32),
            jax.ShapeDtypeStruct((groups * span,), jnp.int32),
        ],
        in_specs=[smem, smem],
        out_specs=[smem, smem],
        name="index_slots",
    )(tile_pairs.T, tile_counts)


def halves(value):
    high = value.astype(BF16)
    low = (value - high.astype(F32)).astype(BF16)
    return high, low


def stacked(value):
    return jnp.concatenate(halves(value), 1)


def product(high, low, both):
    wide = jnp.dot(high, both, preferred_element_type=F32)
    wide = wide + jnp.dot(low, both, preferred_element_type=F32)
    width = both.shape[1] // 2
    return wide[:, :width] + wide[:, width:]


def filter_kernel(n, m, with_gram, x_ref, before_ref, last_ref, ham_ref, *refs):
    if with_gram:
        f_ref, g_ref, *refs = refs
    else:
        f_ref, *refs = refs
    (tiles, fwd_h, fwd_l, back_h, back_l, both, acc, x1_ref, x2_ref, in_x, in_b, out_b) = refs[:12]
    (load_sem, xs_sem, xr_sem, bs_sem, br_sem) = refs[12:17]
    me = lax.axis_index("domain")
    mine = lax.axis_index("vec")
    rows, width = x_ref.shape
    groups = rows // TILE
    span = (REACH + 1) * groups

    load = pltpu.make_async_copy(ham_ref, tiles, load_sem)
    load.start()

    barrier = pltpu.get_barrier_semaphore()
    if with_gram:
        for d in range(1, n):
            pl.semaphore_signal(barrier, inc=1, device_id={"domain": (me + d) % n})
        for d in range(1, m):
            pl.semaphore_signal(barrier, inc=1, device_id={"vec": (mine + d) % m})
        pl.semaphore_wait(barrier, n - 1 + m - 1)
    else:
        for d in range(1, REACH + 1):

            @pl.when(me >= d)
            def _():
                pl.semaphore_signal(barrier, inc=1, device_id={"domain": me - d})

            @pl.when(me + d < n)
            def _():
                pl.semaphore_signal(barrier, inc=1, device_id={"domain": me + d})

        for d in range(1, REACH + 1):

            @pl.when(me >= d)
            def _():
                pl.semaphore_wait(barrier, 1)

            @pl.when(me + d < n)
            def _():
                pl.semaphore_wait(barrier, 1)

    def rows_at(group):
        return pl.ds(group * TILE, TILE)

    sources = (x_ref, x1_ref, x2_ref)

    def x_copy(step, d, group):
        return pltpu.make_async_remote_copy(
            src_ref=sources[step].at[rows_at(group)],
            dst_ref=in_x.at[step, d - 1, rows_at(group)],
            send_sem=xs_sem.at[step, d - 1, group],
            recv_sem=xr_sem.at[step, d - 1, group],
            device_id={"domain": me - d},
        )

    def b_copy(step, d, group):
        return pltpu.make_async_remote_copy(
            src_ref=out_b.at[step, d - 1, rows_at(group)],
            dst_ref=in_b.at[step, d - 1, rows_at(group)],
            send_sem=bs_sem.at[step, d - 1, group],
            recv_sem=br_sem.at[step, d - 1, group],
            device_id={"domain": me + d},
        )

    def send_x(step, group):
        for d in range(1, REACH + 1):

            @pl.when(me >= d)
            def _():
                x_copy(step, d, group).start()

    if with_gram:
        (in_f, part, in_g1, out_g, in_g2, g_mine) = refs[17:23]
        (fs_sem, fr_sem, g1s_sem, g1r_sem, g2s_sem, g2r_sem, hs_sem, hr_sem, ks_sem, kr_sem) = refs[23:]
        far = (mine + 2) % 4
        near = mine + 1 - 2 * (mine % 2)
        cross = (near + 2) % 4

        def f_copy(index, group):
            source = in_f.at[0] if index == 2 else f_ref
            return pltpu.make_async_remote_copy(
                src_ref=source.at[rows_at(group)],
                dst_ref=in_f.at[index, rows_at(group)],
                send_sem=fs_sem.at[index, group],
                recv_sem=fr_sem.at[index, group],
                device_id={"vec": far if index == 0 else near},
            )

    for group in range(groups):
        send_x(0, group)

    both[...] = stacked(x_ref[...])
    load.wait()

    def add_before(slot, carry):
        before = before_ref[slot]
        weight = (before >= 0).astype(F32)
        tiles[slot] = tiles[slot] + tiles[jnp.maximum(before, 0)] * weight
        return carry

    lax.fori_loop(0, tiles.shape[0], add_before, 0)

    def block_at(row, col):
        slot = last_ref[row * span + col]
        return tiles[jnp.maximum(slot, 0)] * (slot >= 0).astype(F32)

    def put(high, low, index, row, col, value):
        high[index, rows_at(row), rows_at(col)], low[index, rows_at(row), rows_at(col)] = halves(value)

    for d in range(1, REACH + 1):
        for row in range(groups):
            for col in range(groups):
                block = block_at(row, d * groups + col)
                put(fwd_h, fwd_l, d, row, col, block)
                put(back_h, back_l, d - 1, col, row, block.T)
    for row in range(groups):
        for col in range(row, groups):
            block = block_at(row, col)
            if row == col:
                put(fwd_h, fwd_l, 0, row, col, 0.5 * (block + block.T))
            else:
                put(fwd_h, fwd_l, 0, row, col, block)
                put(fwd_h, fwd_l, 0, col, row, block.T)

    for step in range(3):
        if step > 0:
            both[...] = stacked(sources[step][...])
        for d in range(1, REACH + 1):

            @pl.when(me + d < n)
            def _():
                out_b[step, d - 1] = product(back_h[d - 1], back_l[d - 1], both[...])

        for group in range(groups):
            for d in range(1, REACH + 1):

                @pl.when(me + d < n)
                def _():
                    b_copy(step, d, group).start()

        acc[...] = product(fwd_h[0], fwd_l[0], both[...])
        for d in range(1, REACH + 1):

            @pl.when(me + d < n)
            def _():
                for group in range(groups):
                    x_copy(step, d, group).wait_recv()
                acc[...] += product(fwd_h[d], fwd_l[d], stacked(in_x[step, d - 1]))

        for group in range(groups):
            here = rows_at(group)
            for d in range(1, REACH + 1):

                @pl.when(me >= d)
                def _():
                    b_copy(step, d, group).wait_recv()
                    acc[here] += in_b[step, d - 1, here]

            if step == 0:
                x1_ref[here] = (acc[here] - center_shift * x_ref[here]) / half_width
            elif step == 1:
                x2_ref[here] = 2.0 * (acc[here] - center_shift * x1_ref[here]) / half_width - x_ref[here]
            else:
                f_ref[here] = 2.0 * (acc[here] - center_shift * x2_ref[here]) / half_width - x1_ref[here]
            if step < 2:
                send_x(step + 1, group)
            elif with_gram:
                f_copy(0, group).start()
                f_copy(1, group).start()

    if with_gram:
        left_h, left_l = halves(f_ref[...].T)
        back_h[0, :width], back_l[0, :width] = left_h, left_l
        total = rows * n

        def gram_block(value, owner):
            block = product(back_h[0, :width], back_l[0, :width], stacked(value)) / total
            part[:, pl.ds(pl.multiple_of(owner * width, width), width)] = block

        for group in range(groups):
            f_copy(0, group).wait_recv()
            f_copy(2, group).start()
        gram_block(f_ref[...], mine)
        for group in range(groups):
            f_copy(1, group).wait_recv()
        gram_block(in_f[1], near)
        gram_block(in_f[0], far)
        for group in range(groups):
            f_copy(2, group).wait_recv()
        gram_block(in_f[2], cross)

        piece = width // n
        pairs = n // 2
        pair = me // 2
        side = me % 2
        mate = me + 1 - 2 * side

        def rows_of(owner):
            return pl.ds(pl.multiple_of(owner * piece, piece), piece)

        def g1_copy(d):
            return pltpu.make_async_remote_copy(
                src_ref=part.at[rows_of(2 * ((pair + d) % pairs) + 1 - side)],
                dst_ref=in_g1.at[d],
                send_sem=g1s_sem.at[d],
                recv_sem=g1r_sem.at[d],
                device_id={"domain": mate},
            )

        def g2_copy(d):
            return pltpu.make_async_remote_copy(
                src_ref=out_g.at[d],
                dst_ref=in_g2.at[d],
                send_sem=g2s_sem.at[d],
                recv_sem=g2r_sem.at[d],
                device_id={"domain": 2 * ((pair + d) % pairs) + side},
            )

        def h_copy(d):
            return pltpu.make_async_remote_copy(
                src_ref=g_mine,
                dst_ref=g_ref.at[rows_of(me)],
                send_sem=hs_sem.at[d],
                recv_sem=hr_sem.at[d],
                device_id={"domain": 2 * ((pair + d) % pairs) + side},
            )

        def k_copy(d):
            owned = rows_of(2 * ((pair + pairs - d) % pairs) + side)
            return pltpu.make_async_remote_copy(
                src_ref=g_mine if d == 0 else g_ref.at[owned],
                dst_ref=g_ref.at[owned],
                send_sem=ks_sem.at[d],
                recv_sem=kr_sem.at[d],
                device_id={"domain": mate},
            )

        order = list(range(1, pairs)) + [0]
        for d in order:
            g1_copy(d).start()
        for d in order:
            g1_copy(d).wait_recv()
            block = part[rows_of(2 * ((pair + d) % pairs) + side)] + in_g1[d]
            if d > 0:
                out_g[d] = block
                g2_copy(d).start()
        for d in range(1, pairs):
            g2_copy(d).wait_recv()
            block = block + in_g2[d]
        g_mine[...] = block
        for d in range(1, pairs):
            h_copy(d).start()
        k_copy(0).start()
        g_ref[rows_of(me)] = block
        for d in range(1, pairs):
            h_copy(d).wait_recv()
            k_copy(d).start()
        for d in range(pairs):
            k_copy(d).wait_recv()
        for group in range(groups):
            for index in range(3):
                f_copy(index, group).wait_send()
        for d in range(pairs):
            g1_copy(d).wait_send()
            k_copy(d).wait_send()
        for d in range(1, pairs):
            g2_copy(d).wait_send()
            h_copy(d).wait_send()

    for step in range(3):
        for d in range(1, REACH + 1):

            @pl.when(me >= d)
            def _():
                for group in range(groups):
                    x_copy(step, d, group).wait_send()

            @pl.when(me + d < n)
            def _():
                for group in range(groups):
                    b_copy(step, d, group).wait_send()


def shards(vectors, hamiltonian, tile_pairs, tile_counts):
    n = lax.axis_size("domain")
    m = lax.axis_size("vec")
    rows, width = vectors.shape
    groups = rows // TILE
    before, last = index_slots(tile_pairs, tile_counts, groups)
    with_gram = m == 4 and n % 2 == 0 and width % (8 * n) == 0
    dma = pltpu.SemaphoreType.DMA
    out_shape = [jax.ShapeDtypeStruct((rows, width), F32)]
    scratch = [
        pltpu.VMEM(hamiltonian.shape, F32),
        pltpu.VMEM((REACH + 1, rows, rows), BF16),
        pltpu.VMEM((REACH + 1, rows, rows), BF16),
        pltpu.VMEM((REACH, rows, rows), BF16),
        pltpu.VMEM((REACH, rows, rows), BF16),
        pltpu.VMEM((rows, 2 * width), BF16),
        pltpu.VMEM((rows, width), F32),
        pltpu.VMEM((rows, width), F32),
        pltpu.VMEM((rows, width), F32),
        pltpu.VMEM((3, REACH, rows, width), F32),
        pltpu.VMEM((3, REACH, rows, width), F32),
        pltpu.VMEM((3, REACH, rows, width), F32),
        dma,
        dma((3, REACH, groups)),
        dma((3, REACH, groups)),
        dma((3, REACH, groups)),
        dma((3, REACH, groups)),
    ]
    if with_gram:
        out_shape.append(jax.ShapeDtypeStruct((width, m * width), F32))
        scratch += [
            pltpu.VMEM((3, rows, width), F32),
            pltpu.VMEM((width, m * width), F32),
            pltpu.VMEM((n // 2, width // n, m * width), F32),
            pltpu.VMEM((n // 2, width // n, m * width), F32),
            pltpu.VMEM((n // 2, width // n, m * width), F32),
            pltpu.VMEM((width // n, m * width), F32),
            dma((3, groups)),
            dma((3, groups)),
        ]
        scratch += [dma((n // 2,))] * 8
    outs = pl.pallas_call(
        functools.partial(filter_kernel, n, m, with_gram),
        out_shape=out_shape,
        in_specs=[
            pl.BlockSpec(memory_space=pltpu.VMEM),
            pl.BlockSpec(memory_space=pltpu.SMEM),
            pl.BlockSpec(memory_space=pltpu.SMEM),
            pl.BlockSpec(memory_space=pl.ANY),
        ],
        out_specs=[pl.BlockSpec(memory_space=pltpu.VMEM)] * len(out_shape),
        scratch_shapes=scratch,
        compiler_params=pltpu.CompilerParams(
            collective_id=0, has_side_effects=True, vmem_limit_bytes=62 * 2**20
        ),
        name="chebyshev",
    )(vectors, before, last, hamiltonian)
    if with_gram:
        return tuple(outs)
    (filtered,) = outs
    gathered = lax.all_gather(filtered, "vec", axis=1, tiled=True)
    partial_block = jnp.dot(
        filtered.T, gathered, precision=lax.Precision.HIGHEST, preferred_element_type=F32
    ) / (rows * n)
    return (filtered, lax.psum(partial_block, "domain"))


def solution(mesh):
    in_specs = (P("domain", "vec"), P("domain", None, None), P("domain", None), P("domain"))
    out_specs = (P("domain", "vec"), P("vec", None))
    return jax.shard_map(shards, mesh=mesh, in_specs=in_specs, out_specs=out_specs, check_vma=False)
```

time: 79.6 us -> 75.9 us (0.954); the launches traced: 78.3 us -> 75.7 us
  local copies, waits for them, and re-layouts: 4.68 us -> 3.34 us
  Pallas kernels: 72.2 us -> 71 us
    pallas_call x1, Pallas kernels: 4.58 us -> 1.95 us  [index_slots(): pl.pallas_call(functools.partial(index_kernel, groups, span), out_shape=[...]
    pallas_call x1, Pallas kernels: 67.6 us -> 69.1 us  [shards(): pl.pallas_call(functools.partial(filter_kernel, n, m, with_gram), out_sha...]
    unnamed x7 -> x2, local copies, waits for them, and re-layouts: 4.68 us -> 3.34 us
where the time goes in v2:
time: 75.9 us; the launch traced here: 75.7 us
  Pallas kernels  71 us (94%)
  local copies, waits for them, and re-layouts  3.34 us (4%)
  between operations  1.29 us (2%)
    pallas_call x1, Pallas kernels, shards(): pl.pallas_call(functools.partial(filter_kernel, n, m, with_gram), out_sha...  69.1 us
    unnamed x2, local copies, waits for them, and re-layouts  3.34 us
    pallas_call x1, Pallas kernels, index_slots(): pl.pallas_call(functools.partial(index_kernel, groups, span), out_shape=[...  1.95 us

profile of v2, /device:TPU:0, one launch (start us, length us, event | category | flops | bytes accessed | tf_op | source)
XLA Modules:
  0.0 75.7 jit_solution(9917005029304219792)
XLA Ops:
  1.3 1.9 %index_slots.1 = (s32[64]{0:T(128)}, s32[48]{0:T(128)}) custom-call(s32[2,64]{1,0:T(2,128)} %bitcast.1, s32[1]{0:T(128)S(6)} %copy.8.count_ref), custom_call_target="tpu_custom_call" | custom-call | tf_op jit(solution)/shard_map/index_slots/pallas_call | solution.py:47
  3.2 69.1 %chebyshev.1 = (f32[512,128]{1,0:T(8,128)}, f32[128,512]{1,0:T(8,128)}) custom-call(f32[512,128]{1,0:T(8,128)} %x_ref.1, s32[64]{0:T(128)} %get-tuple-element.4.before_ref, s32[48]{0:T(128)} %get-tuple-element.5.last_ref, f32[64,128,128]{2,1,0:T(8,128)} %ham_ref.1), custom_call_target="tpu_custom_call" | custom-call | tf_op jit(solution)/shard_map/chebyshev/pallas_call | solution.py:403
  72.3 1.7 %copy.9 = f32[512,128]{1,0:T(8,128)} copy(f32[512,128]{1,0:T(8,128)} %get-tuple-element.8) | data formatting | bytes 524288
  74.0 1.7 %copy.10 = f32[128,512]{1,0:T(8,128)} copy(f32[128,512]{1,0:T(8,128)} %get-tuple-element.9) | data formatting | bytes 524288

commit v3 on v2

--- a/solution.py
+++ b/solution.py
@@ -148,8 +148,8 @@
                 x_copy(step, d, group).start()
 
     if with_gram:
-        (in_f, part, in_g1, out_g, in_g2, g_mine) = refs[17:23]
-        (fs_sem, fr_sem, g1s_sem, g1r_sem, g2s_sem, g2r_sem, hs_sem, hr_sem, ks_sem, kr_sem) = refs[23:]
+        (in_f, part, in_g1, out_g, in_g2, in_h, in_k) = refs[17:24]
+        (fs_sem, fr_sem, g1s_sem, g1r_sem, g2s_sem, g2r_sem, hs_sem, hr_sem, ks_sem, kr_sem) = refs[24:]
         far = (mine + 2) % 4
         near = mine + 1 - 2 * (mine % 2)
         cross = (near + 2) % 4
@@ -251,99 +251,129 @@
         back_h[0, :width], back_l[0, :width] = left_h, left_l
         total = rows * n
 
-        def gram_block(value, owner):
-            block = product(back_h[0, :width], back_l[0, :width], stacked(value)) / total
-            part[:, pl.ds(pl.multiple_of(owner * width, width), width)] = block
-
-        for group in range(groups):
-            f_copy(0, group).wait_recv()
-            f_copy(2, group).start()
-        gram_block(f_ref[...], mine)
-        for group in range(groups):
-            f_copy(1, group).wait_recv()
-        gram_block(in_f[1], near)
-        gram_block(in_f[0], far)
-        for group in range(groups):
-            f_copy(2, group).wait_recv()
-        gram_block(in_f[2], cross)
-
         piece = width // n
         pairs = n // 2
         pair = me // 2
         side = me % 2
         mate = me + 1 - 2 * side
+        owners = (mine, near, far, cross)
 
         def rows_of(owner):
             return pl.ds(pl.multiple_of(owner * piece, piece), piece)
 
-        def g1_copy(d):
+        def at(column, owner):
+            return (rows_of(owner), pl.ds(pl.multiple_of(owners[column] * width, width), width))
+
+        def g1_copy(column, d):
             return pltpu.make_async_remote_copy(
-                src_ref=part.at[rows_of(2 * ((pair + d) % pairs) + 1 - side)],
-                dst_ref=in_g1.at[d],
-                send_sem=g1s_sem.at[d],
-                recv_sem=g1r_sem.at[d],
+                src_ref=part.at[column, rows_of(2 * ((pair + d) % pairs) + 1 - side)],
+                dst_ref=in_g1.at[column, d],
+                send_sem=g1s_sem.at[column, d],
+                recv_sem=g1r_sem.at[column, d],
                 device_id={"domain": mate},
             )
 
-        def g2_copy(d):
+        def g2_copy(column, d):
             return pltpu.make_async_remote_copy(
-                src_ref=out_g.at[d],
-                dst_ref=in_g2.at[d],
-                send_sem=g2s_sem.at[d],
-                recv_sem=g2r_sem.at[d],
+                src_ref=out_g.at[column, d],
+                dst_ref=in_g2.at[column, d],
+                send_sem=g2s_sem.at[column, d],
+                recv_sem=g2r_sem.at[column, d],
                 device_id={"domain": 2 * ((pair + d) % pairs) + side},
             )
 
-        def h_copy(d):
+        def h_copy(column, d):
             return pltpu.make_async_remote_copy(
-                src_ref=g_mine,
-                dst_ref=g_ref.at[rows_of(me)],
-                send_sem=hs_sem.at[d],
-                recv_sem=hr_sem.at[d],
+                src_ref=out_g.at[column, 0],
+                dst_ref=in_h.at[column, d],
+                send_sem=hs_sem.at[column, d],
+                recv_sem=hr_sem.at[column, d],
                 device_id={"domain": 2 * ((pair + d) % pairs) + side},
             )
 
-        def k_copy(d):
-            owned = rows_of(2 * ((pair + pairs - d) % pairs) + side)
+        def k_copy(column, d):
             return pltpu.make_async_remote_copy(
-                src_ref=g_mine if d == 0 else g_ref.at[owned],
-                dst_ref=g_ref.at[owned],
-                send_sem=ks_sem.at[d],
-                recv_sem=kr_sem.at[d],
+                src_ref=out_g.at[column, 0] if d == 0 else in_h.at[column, d],
+                dst_ref=in_k.at[column, d],
+                send_sem=ks_sem.at[column, d],
+                recv_sem=kr_sem.at[column, d],
                 device_id={"domain": mate},
             )
 
         order = list(range(1, pairs)) + [0]
-        for d in order:
-            g1_copy(d).start()
-        for d in order:
-            g1_copy(d).wait_recv()
-            block = part[rows_of(2 * ((pair + d) % pairs) + side)] + in_g1[d]
-            if d > 0:
-                out_g[d] = block
-                g2_copy(d).start()
-        for d in range(1, pairs):
-            g2_copy(d).wait_recv()
-            block = block + in_g2[d]
-        g_mine[...] = block
-        for d in range(1, pairs):
-            h_copy(d).start()
-        k_copy(0).start()
-        g_ref[rows_of(me)] = block
-        for d in range(1, pairs):
-            h_copy(d).wait_recv()
-            k_copy(d).start()
-        for d in range(pairs):
-            k_copy(d).wait_recv()
+
+        def multiply(column, value):
+            block = product(back_h[0, :width], back_l[0, :width], stacked(value)) / total
+            part[column] = block
+            for d in order:
+                g1_copy(column, d).start()
+
+        def add_mate(column):
+            for d in order:
+                g1_copy(column, d).wait_recv()
+                out_g[column, d] = part[column, rows_of(2 * ((pair + d) % pairs) + side)] + in_g1[column, d]
+                if d > 0:
+                    g2_copy(column, d).start()
+
+        def add_pairs(column):
+            block = out_g[column, 0]
+            for d in range(1, pairs):
+                g2_copy(column, d).wait_recv()
+                block = block + in_g2[column, d]
+            out_g[column, 0] = block
+            for d in range(1, pairs):
+                h_copy(column, d).start()
+            k_copy(column, 0).start()
+            g_ref[at(column, me)] = block
+
+        def from_pairs(column):
+            for d in range(1, pairs):
+                h_copy(column, d).wait_recv()
+                k_copy(column, d).start()
+                g_ref[at(column, 2 * ((pair + pairs - d) % pairs) + side)] = in_h[column, d]
+
+        def from_mate(column):
+            for d in range(pairs):
+                k_copy(column, d).wait_recv()
+                g_ref[at(column, 2 * ((pair + pairs - d) % pairs) + 1 - side)] = in_k[column, d]
+
+        multiply(0, f_ref[...])
+        for group in range(groups):
+            f_copy(1, group).wait_recv()
+        multiply(1, in_f[1])
+        for group in range(groups):
+            f_copy(0, group).wait_recv()
+            f_copy(2, group).start()
+        multiply(2, in_f[0])
+        add_mate(0)
+        add_mate(1)
+        for group in range(groups):
+            f_copy(2, group).wait_recv()
+        multiply(3, in_f[2])
+        add_mate(2)
+        add_pairs(0)
+        add_pairs(1)
+        add_mate(3)
+        add_pairs(2)
+        from_pairs(0)
+        from_pairs(1)
+        add_pairs(3)
+        from_pairs(2)
+        from_mate(0)
+        from_mate(1)
+        from_pairs(3)
+        from_mate(2)
+        from_mate(3)
         for group in range(groups):
             for index in range(3):
                 f_copy(index, group).wait_send()
-        for d in range(pairs):
-            g1_copy(d).wait_send()
-            k_copy(d).wait_send()
-        for d in range(1, pairs):
-            g2_copy(d).wait_send()
-            h_copy(d).wait_send()
+        for column in range(4):
+            for d in range(pairs):
+                g1_copy(column, d).wait_send()
+                k_copy(column, d).wait_send()
+            for d in range(1, pairs):
+                g2_copy(column, d).wait_send()
+                h_copy(column, d).wait_send()
 
     for step in range(3):
         for d in range(1, REACH + 1):
@@ -391,15 +421,12 @@
         out_shape.append(jax.ShapeDtypeStruct((width, m * width), F32))
         scratch += [
             pltpu.VMEM((3, rows, width), F32),
-            pltpu.VMEM((width, m * width), F32),
-            pltpu.VMEM((n // 2, width // n, m * width), F32),
-            pltpu.VMEM((n // 2, width // n, m * width), F32),
-            pltpu.VMEM((n // 2, width // n, m * width), F32),
-            pltpu.VMEM((width // n, m * width), F32),
+            pltpu.VMEM((m, width, width), F32),
             dma((3, groups)),
             dma((3, groups)),
         ]
-        scratch += [dma((n // 2,))] * 8
+        scratch[-2:-2] = [pltpu.VMEM((m, n // 2, width // n, width), F32)] * 5
+        scratch += [dma((m, n // 2))] * 8
     outs = pl.pallas_call(
         functools.partial(filter_kernel, n, m, with_gram),
         out_shape=out_shape,
@@ -412,7 +439,7 @@
         out_specs=[pl.BlockSpec(memory_space=pltpu.VMEM)] * len(out_shape),
         scratch_shapes=scratch,
         compiler_params=pltpu.CompilerParams(
-            collective_id=0, has_side_effects=True, vmem_limit_bytes=62 * 2**20
+            collective_id=0, has_side_effects=True, vmem_limit_bytes=52 * 2**20
         ),
         name="chebyshev",
     )(vectors, before, last, hamiltonian)

time: 75.9 us -> 74.6 us (0.983)
  Pallas kernels: 71 us -> 69.4 us
    pallas_call x1, Pallas kernels: 69.1 us -> 67.3 us  [shards(): pl.pallas_call(functools.partial(filter_kernel, n, m, with_gram), out_sha...]
    unnamed x2 -> x8, local copies, waits for them, and re-layouts: 3.34 us -> 3.66 us
where the time goes in v3:
time: 74.6 us; the launch traced here: 74.3 us
  Pallas kernels  69.4 us (93%)
  local copies, waits for them, and re-layouts  3.66 us (5%)
  between operations  1.3 us (2%)
    pallas_call x1, Pallas kernels, shards(): pl.pallas_call(functools.partial(filter_kernel, n, m, with_gram), out_sha...  67.3 us
    unnamed x8, local copies, waits for them, and re-layouts  3.66 us
    pallas_call x1, Pallas kernels, index_slots(): pl.pallas_call(functools.partial(index_kernel, groups, span), out_shape=[...  2.05 us

profile of v3, /device:TPU:0, one launch (start us, length us, event | category | flops | bytes accessed | tf_op | source)
XLA Modules:
  0.0 74.3 jit_solution(16046646481381022352)
XLA Ops:
  1.3 2.1 %index_slots.1 = (s32[64]{0:T(128)}, s32[48]{0:T(128)}) custom-call(s32[2,64]{1,0:T(2,128)} %bitcast.1, s32[1]{0:T(128)S(6)} %copy.8.count_ref), custom_call_target="tpu_custom_call" | custom-call | tf_op jit(solution)/shard_map/index_slots/pallas_call | solution.py:47
  3.3 0.0 copy-start
  3.3 0.9 %copy-done = f32[512,128]{1,0:T(8,128)S(1)} copy-done((f32[512,128]{1,0:T(8,128)S(1)}, f32[512,128]{1,0:T(8,128)}, u32[]{:S(2)}) %copy-start) | copy-done | bytes 262168
  4.3 0.0 copy-start.1
  4.3 0.7 copy-done.1
  4.9 0.0 copy-start.2
  4.9 0.7 copy-done.2
  5.6 67.3 %chebyshev.1 = (f32[512,128]{1,0:T(8,128)S(1)}, f32[128,512]{1,0:T(8,128)S(1)}) custom-call(f32[512,128]{1,0:T(8,128)S(1)} %copy-done, s32[64]{0:T(128)S(1)} %copy-done.1, s32[48]{0:T(128)S(1)} %copy-done.2, f32[64,128,128]{2,1,0:T(8,128)} %ham_ref.1), custom_call_target="tpu_custom_call" | custom-call | tf_op jit(solution)/shard_map/chebyshev/pallas_call | solution.py:430
  72.9 0.7 copy.9
  73.6 0.7 copy.10
Async XLA Ops:
  3.3 1.0 %copy-start = (f32[512,128]{1,0:T(8,128)S(1)}, f32[512,128]{1,0:T(8,128)}, u32[]{:S(2)}) copy-start(f32[512,128]{1,0:T(8,128)} %x_ref.1) | copy-start | bytes 786436
  4.3 0.7 copy-start.1
  4.9 0.7 copy-start.2

commit v4 on v3

--- a/solution.py
+++ b/solution.py
@@ -140,10 +140,25 @@
             device_id={"domain": me + d},
         )
 
+    relayed = n % 2 == 0 and REACH == 2
+    even = me % 2 == 0
+
+    def x_relay(step, group):
+        return pltpu.make_async_remote_copy(
+            src_ref=in_x.at[step, 1, rows_at(group)],
+            dst_ref=in_x.at[step, 0, rows_at(group)],
+            send_sem=xs_sem.at[step, 0, group],
+            recv_sem=xr_sem.at[step, 0, group],
+            device_id={"domain": me + 1},
+        )
+
+    def sends_x(d):
+        return jnp.logical_and(me >= d, me % 2 == 1) if relayed and d == 1 else me >= d
+
     def send_x(step, group):
         for d in range(1, REACH + 1):
 
-            @pl.when(me >= d)
+            @pl.when(sends_x(d))
             def _():
                 x_copy(step, d, group).start()
 
@@ -209,20 +224,38 @@
             def _():
                 out_b[step, d - 1] = product(back_h[d - 1], back_l[d - 1], both[...])
 
-        for group in range(groups):
-            for d in range(1, REACH + 1):
-
-                @pl.when(me + d < n)
-                def _():
-                    b_copy(step, d, group).start()
-
+        def send_back(first, last):
+            for group in range(first, last):
+                for d in range(1, REACH + 1):
+
+                    @pl.when(me + d < n)
+                    def _():
+                        b_copy(step, d, group).start()
+
+        send_back(0, groups // 2)
         acc[...] = product(fwd_h[0], fwd_l[0], both[...])
-        for d in range(1, REACH + 1):
-
-            @pl.when(me + d < n)
+        if relayed:
+
+            @pl.when(jnp.logical_and(even, me + 2 < n))
+            def _():
+                for group in range(groups):
+                    x_copy(step, 2, group).wait_recv()
+                    x_relay(step, group).start()
+
+        send_back(groups // 2, groups)
+        for d in range(REACH, 0, -1):
+            if relayed and d == 2:
+                waits = jnp.logical_and(me % 2 == 1, me + d < n)
+            else:
+                waits = me + d < n
+
+            @pl.when(waits)
             def _():
                 for group in range(groups):
                     x_copy(step, d, group).wait_recv()
+
+            @pl.when(me + d < n)
+            def _():
                 acc[...] += product(fwd_h[d], fwd_l[d], stacked(in_x[step, d - 1]))
 
         for group in range(groups):
@@ -376,9 +409,16 @@
                 h_copy(column, d).wait_send()
 
     for step in range(3):
+        if relayed:
+
+            @pl.when(jnp.logical_and(even, me + 2 < n))
+            def _():
+                for group in range(groups):
+                    x_relay(step, group).wait_send()
+
         for d in range(1, REACH + 1):
 
-            @pl.when(me >= d)
+            @pl.when(sends_x(d))
             def _():
                 for group in range(groups):
                     x_copy(step, d, group).wait_send()

time: 74.6 us -> 75.6 us (1.013)
  Pallas kernels: 69.4 us -> 70.5 us
    pallas_call x1, Pallas kernels: 67.3 us -> 68.5 us  [shards(): pl.pallas_call(functools.partial(filter_kernel, n, m, with_gram), out_sha...]
where the time goes in v4:
time: 75.6 us; the launch traced here: 75.5 us
  Pallas kernels  70.5 us (93%)
  local copies, waits for them, and re-layouts  3.66 us (5%)
  between operations  1.3 us (2%)
    pallas_call x1, Pallas kernels, shards(): pl.pallas_call(functools.partial(filter_kernel, n, m, with_gram), out_sha...  68.5 us
    unnamed x8, local copies, waits for them, and re-layouts  3.66 us
    pallas_call x1, Pallas kernels, index_slots(): pl.pallas_call(functools.partial(index_kernel, groups, span), out_shape=[...  2.03 us

profile of v4, /device:TPU:0, one launch (start us, length us, event | category | flops | bytes accessed | tf_op | source)
XLA Modules:
  0.0 75.5 jit_solution(6859412467988137677)
XLA Ops:
  1.3 2.0 %index_slots.1 = (s32[64]{0:T(128)}, s32[48]{0:T(128)}) custom-call(s32[2,64]{1,0:T(2,128)} %bitcast.1, s32[1]{0:T(128)S(6)} %copy.8.count_ref), custom_call_target="tpu_custom_call" | custom-call | tf_op jit(solution)/shard_map/index_slots/pallas_call | solution.py:47
  3.3 0.0 copy-start
  3.3 0.9 %copy-done = f32[512,128]{1,0:T(8,128)S(1)} copy-done((f32[512,128]{1,0:T(8,128)S(1)}, f32[512,128]{1,0:T(8,128)}, u32[]{:S(2)}) %copy-start) | copy-done | bytes 262168
  4.3 0.0 copy-start.1
  4.3 0.7 copy-done.1
  4.9 0.0 copy-start.2
  4.9 0.7 copy-done.2
  5.6 68.5 %chebyshev.1 = (f32[512,128]{1,0:T(8,128)S(1)}, f32[128,512]{1,0:T(8,128)S(1)}) custom-call(f32[512,128]{1,0:T(8,128)S(1)} %copy-done, s32[64]{0:T(128)S(1)} %copy-done.1, s32[48]{0:T(128)S(1)} %copy-done.2, f32[64,128,128]{2,1,0:T(8,128)} %ham_ref.1), custom_call_target="tpu_custom_call" | custom-call | tf_op jit(solution)/shard_map/chebyshev/pallas_call | solution.py:470
  74.1 0.7 copy.9
  74.8 0.7 copy.10
Async XLA Ops:
  3.3 1.0 %copy-start = (f32[512,128]{1,0:T(8,128)S(1)}, f32[512,128]{1,0:T(8,128)}, u32[]{:S(2)}) copy-start(f32[512,128]{1,0:T(8,128)} %x_ref.1) | copy-start | bytes 786436
  4.3 0.7 copy-start.1
  4.9 0.7 copy-start.2

commit v5 on v3

--- a/solution.py
+++ b/solution.py
@@ -140,12 +140,15 @@
             device_id={"domain": me + d},
         )
 
-    def send_x(step, group):
-        for d in range(1, REACH + 1):
-
-            @pl.when(me >= d)
-            def _():
-                x_copy(step, d, group).start()
+    def send_x(step, d, group):
+        @pl.when(me >= d)
+        def _():
+            x_copy(step, d, group).start()
+
+    def send_x_far(step):
+        for d in range(2, REACH + 1):
+            for group in range(groups):
+                send_x(step, d, group)
 
     if with_gram:
         (in_f, part, in_g1, out_g, in_g2, in_h, in_k) = refs[17:24]
@@ -165,7 +168,8 @@
             )
 
     for group in range(groups):
-        send_x(0, group)
+        send_x(0, 1, group)
+    send_x_far(0)
 
     both[...] = stacked(x_ref[...])
     load.wait()
@@ -241,10 +245,12 @@
             else:
                 f_ref[here] = 2.0 * (acc[here] - center_shift * x2_ref[here]) / half_width - x1_ref[here]
             if step < 2:
-                send_x(step + 1, group)
+                send_x(step + 1, 1, group)
             elif with_gram:
                 f_copy(0, group).start()
                 f_copy(1, group).start()
+        if step < 2:
+            send_x_far(step + 1)
 
     if with_gram:
         left_h, left_l = halves(f_ref[...].T)

time: 74.6 us -> 74.4 us (level)
  no operation moved by 1% of the time
where the time goes in v5:
time: 74.4 us; the launch traced here: 74.2 us
  Pallas kernels  69.3 us (93%)
  local copies, waits for them, and re-layouts  3.66 us (5%)
  between operations  1.3 us (2%)
    pallas_call x1, Pallas kernels, shards(): pl.pallas_call(functools.partial(filter_kernel, n, m, with_gram), out_sha...  67.3 us
    unnamed x8, local copies, waits for them, and re-layouts  3.66 us
    pallas_call x1, Pallas kernels, index_slots(): pl.pallas_call(functools.partial(index_kernel, groups, span), out_shape=[...  1.98 us

profile of v5, /device:TPU:0, one launch (start us, length us, event | category | flops | bytes accessed | tf_op | source)
XLA Modules:
  0.0 74.2 jit_solution(7835344790604644081)
XLA Ops:
  1.3 2.0 %index_slots.1 = (s32[64]{0:T(128)}, s32[48]{0:T(128)}) custom-call(s32[2,64]{1,0:T(2,128)} %bitcast.1, s32[1]{0:T(128)S(6)} %copy.8.count_ref), custom_call_target="tpu_custom_call" | custom-call | tf_op jit(solution)/shard_map/index_slots/pallas_call | solution.py:47
  3.3 0.0 copy-start
  3.3 0.9 %copy-done = f32[512,128]{1,0:T(8,128)S(1)} copy-done((f32[512,128]{1,0:T(8,128)S(1)}, f32[512,128]{1,0:T(8,128)}, u32[]{:S(2)}) %copy-start) | copy-done | bytes 262168
  4.2 0.0 copy-start.1
  4.2 0.7 copy-done.1
  4.9 0.0 copy-start.2
  4.9 0.7 copy-done.2
  5.5 67.3 %chebyshev.1 = (f32[512,128]{1,0:T(8,128)S(1)}, f32[128,512]{1,0:T(8,128)S(1)}) custom-call(f32[512,128]{1,0:T(8,128)S(1)} %copy-done, s32[64]{0:T(128)S(1)} %copy-done.1, s32[48]{0:T(128)S(1)} %copy-done.2, f32[64,128,128]{2,1,0:T(8,128)} %ham_ref.1), custom_call_target="tpu_custom_call" | custom-call | tf_op jit(solution)/shard_map/chebyshev/pallas_call | solution.py:436
  72.8 0.7 copy.9
  73.5 0.7 copy.10
Async XLA Ops:
  3.3 1.0 %copy-start = (f32[512,128]{1,0:T(8,128)S(1)}, f32[512,128]{1,0:T(8,128)}, u32[]{:S(2)}) copy-start(f32[512,128]{1,0:T(8,128)} %x_ref.1) | copy-start | bytes 786436
  4.2 0.7 copy-start.1
  4.9 0.7 copy-start.2
